TPU v7x, 32 devices: a whole 2x2x4 slice. The times are simulated.
32 devices in a mesh: dp: 4 (over z), seqhi: 2 (over x), seqlo: 4 (over y, core).
Axes of the slice: x: 2, y: 2, z: 4, core: 2. Of those that a mesh axis runs over, the one named last changes fastest.
Arguments:
- queries: bfloat16 [4, 2048, 384], P('dp', ('seqhi', 'seqlo')), may hold values from -2 to 2
- key_rows: bfloat16 [4, 2048, 384], P('dp', ('seqhi', 'seqlo')), may hold values from -2 to 2
- value_rows: bfloat16 [4, 2048, 384], P('dp', ('seqhi', 'seqlo')), may hold values from -3 to 3
- head_scale: float32 [6], replicated, may hold values from 0.15 to 1
- out_weight: bfloat16 [384, 384], replicated, may hold values from -0.3125 to 0.3125
- cotangent: bfloat16 [4, 2048, 384], P('dp', ('seqhi', 'seqlo')), may hold values from -6 to 6
Outputs:
- queries_gradient: bfloat16 [4, 2048, 384], P('dp', ('seqhi', 'seqlo'))
- keys_gradient: bfloat16 [4, 2048, 384], P('dp', ('seqhi', 'seqlo'))
- values_gradient: bfloat16 [4, 2048, 384], P('dp', ('seqhi', 'seqlo'))
- weight_gradient: float32 [384, 384], P('dp')
All inputs are finite; a program needn't handle non-finite values.
Results may differ from a plain program's by a relative error of at most 0.025.
Values may be sent and summed in bfloat16 or wider, within the bound.
No kernel may reach another device: no remote copies, remote signals or barrier semaphores. Data moves between devices by JAX's collectives and lax.ppermute only.
A program may use at most 64 MiB of HBM per device.

v0:
```python
import jax
import jax.numpy as jnp
from jax import lax
from jax.sharding import PartitionSpec as P


def swapped(value, axis, stride):
    mask = 2**stride
    pairs = [(source, source ^ mask) for source in range(lax.axis_size(axis))]
    return lax.ppermute(value, axis, pairs)


def split_heads(matrix, head_count):
    return matrix.reshape(matrix.shape[0], head_count, matrix.shape[1] // head_count)


def pair_mean(matrix):
    paired = matrix.astype(jnp.float32).reshape(matrix.shape[0] // 2, 2, matrix.shape[1])
    return (0.5 * (paired[:, 0] + paired[:, 1])).astype(jnp.bfloat16)


def pair_total(matrix):
    paired = matrix.astype(jnp.float32).reshape(matrix.shape[0] // 2, 2, matrix.shape[1])
    return (paired[:, 0] + paired[:, 1]).astype(jnp.bfloat16)


def spread_rows(matrix, factor):
    widened = jnp.broadcast_to(matrix[:, None], (matrix.shape[0], factor) + matrix.shape[1:])
    return widened.reshape((matrix.shape[0] * factor,) + matrix.shape[1:])


def group_sum(matrix, factor):
    return jnp.sum(matrix.reshape((matrix.shape[0] // factor, factor) + matrix.shape[1:]), axis=1)


def score_terms(queries, key_block, scales):
    head_count = scales.shape[0]
    factor = scales / jnp.sqrt(jnp.float32(queries.shape[1] // head_count))
    logits = jnp.einsum(
        "rhe,che->hrc",
        split_heads(queries, head_count),
        split_heads(key_block, head_count),
        preferred_element_type=jnp.float32,
    )
    return (jnp.exp(logits * factor[:, None, None]), factor)


def attend(queries, key_block, value_block, scales, multiplicity):
    head_count = scales.shape[0]
    weights, factor = score_terms(queries, key_block, scales)
    probabilities = weights.astype(jnp.bfloat16)
    numerator = jnp.einsum(
        "hrc,che->rhe",
        probabilities,
        split_heads(value_block, head_count),
        preferred_element_type=jnp.float32,
    )
    numerator = numerator.reshape(queries.shape[0], queries.shape[1])
    denominator = multiplicity * jnp.sum(weights, axis=2).T
    return (numerator, denominator)


def attend_back(queries, key_block, value_block, scales, multiplicity, numer_grad, denom_grad):
    head_count = scales.shape[0]
    weights, factor = score_terms(queries, key_block, scales)
    probabilities = weights.astype(jnp.bfloat16)
    grad_heads = split_heads(numer_grad, head_count)
    prob_grad = jnp.einsum(
        "rhe,che->hrc",
        grad_heads,
        split_heads(value_block, head_count),
        preferred_element_type=jnp.float32,
    )
    logit_grad = (
        weights * (prob_grad + multiplicity * denom_grad.T[:, :, None]) * factor[:, None, None]
    ).astype(jnp.bfloat16)
    query_piece = jnp.einsum(
        "hrc,che->rhe",
        logit_grad,
        split_heads(key_block, head_count),
        preferred_element_type=jnp.float32,
    ).reshape(queries.shape)
    key_piece = jnp.einsum(
        "hrc,rhe->che",
        logit_grad,
        split_heads(queries, head_count),
        preferred_element_type=jnp.float32,
    ).reshape(key_block.shape)
    value_piece = jnp.einsum(
        "hrc,rhe->che", probabilities, grad_heads, preferred_element_type=jnp.float32
    ).reshape(value_block.shape)
    return (query_piece, key_piece, value_piece)


def shards(queries, key_rows, value_rows, head_scale, out_weight, cotangent):
    query_local = queries[0]
    key_local = key_rows[0]
    value_local = value_rows[0]
    cotan_local = cotangent[0]
    head_count = head_scale.shape[0]
    feature_width = query_local.shape[1]
    block_rows = key_local.shape[0] // 2
    top_level = lax.axis_size(("seqhi", "seqlo")).bit_length() - 1
    position = lax.axis_index(("seqhi", "seqlo"))
    numerator, denominator = attend(query_local, key_local, value_local, head_scale, 1.0)
    coarse_queries = [query_local]
    sibling_pairs = [None]
    level_numers = [None]
    level_denoms = [None]
    own_keys = pair_mean(key_local)
    own_values = pair_total(value_local)
    for height in range(1, top_level + 1):
        coarse_queries.append(pair_mean(coarse_queries[-1]))
        if height > 1:
            lower_first = position // 2 ** (height - 2) % 2 == 0
            sib_keys, sib_values = sibling_pairs[-1]
            own_keys = pair_mean(
                jnp.concatenate(
                    [
                        jnp.where(lower_first, own_keys, sib_keys),
                        jnp.where(lower_first, sib_keys, own_keys),
                    ],
                    axis=0,
                )
            )
            own_values = pair_total(
                jnp.concatenate(
                    [
                        jnp.where(lower_first, own_values, sib_values),
                        jnp.where(lower_first, sib_values, own_values),
                    ],
                    axis=0,
                )
            )
        arrived = swapped((own_keys, own_values), ("seqhi", "seqlo"), height - 1)
        sibling_pairs.append(arrived)
        level_numer, level_denom = attend(
            coarse_queries[height], arrived[0], arrived[1], head_scale, float(2**height)
        )
        level_numers.append(level_numer)
        level_denoms.append(level_denom)
    numer_acc = level_numers[top_level]
    denom_acc = level_denoms[top_level]
    for height in range(top_level - 1, 0, -1):
        numer_acc = level_numers[height] + spread_rows(numer_acc, 2)
        denom_acc = level_denoms[height] + spread_rows(denom_acc, 2)
    numerator = numerator + spread_rows(numer_acc, 2)
    denominator = denominator + spread_rows(denom_acc, 2)
    attended_heads = split_heads(numerator, head_count) / denominator[:, :, None]
    attended = attended_heads.reshape(numerator.shape).astype(jnp.bfloat16)
    own_rows = feature_width // lax.axis_size("dp")
    weight_term = lax.dot_general(
        attended, cotan_local, (((0,), (0,)), ((), ())), preferred_element_type=jnp.float32
    )
    summed = lax.psum(weight_term, ("dp", "seqhi", "seqlo"))
    weight_gradient = lax.dynamic_slice_in_dim(summed, lax.axis_index("dp") * own_rows, own_rows, 0)
    backward = lax.dot_general(
        cotan_local, out_weight, (((1,), (1,)), ((), ())), preferred_element_type=jnp.float32
    ).astype(jnp.bfloat16)
    back_heads = split_heads(backward, head_count).astype(jnp.float32)
    numer_grad = (back_heads / denominator[:, :, None]).reshape(numerator.shape)
    denom_grad = -jnp.sum(back_heads * attended_heads, axis=2) / denominator
    query_grad, key_grad, value_grad = attend_back(
        query_local,
        key_local,
        value_local,
        head_scale,
        1.0,
        numer_grad.astype(jnp.bfloat16),
        denom_grad,
    )
    level_query_grads = [None]
    level_key_sends = [None]
    numer_group = numer_grad
    denom_group = denom_grad
    for height in range(1, top_level + 1):
        numer_group = group_sum(numer_group, 2)
        denom_group = group_sum(denom_group, 2)
        query_piece, key_piece, value_piece = attend_back(
            coarse_queries[height],
            sibling_pairs[height][0],
            sibling_pairs[height][1],
            head_scale,
            float(2**height),
            numer_group.astype(jnp.bfloat16),
            denom_group,
        )
        level_query_grads.append(query_piece)
        level_key_sends.append((key_piece, value_piece))
    chain_query = level_query_grads[top_level]
    for height in range(top_level - 1, 0, -1):
        chain_query = level_query_grads[height] + spread_rows(0.5 * chain_query, 2)
    query_total = query_grad + spread_rows(0.5 * chain_query, 2)
    returned = [None]
    for height in range(1, top_level + 1):
        returned.append(swapped(level_key_sends[height], ("seqhi", "seqlo"), height - 1))
    carry_pair = returned[top_level]
    for height in range(top_level - 1, 0, -1):
        up_keys = spread_rows(0.5 * carry_pair[0], 2)
        up_values = spread_rows(carry_pair[1], 2)
        split_lower_first = position // 2 ** (height - 1) % 2 == 0
        own_pair = (
            jnp.where(split_lower_first, up_keys[:block_rows], up_keys[block_rows:]),
            jnp.where(split_lower_first, up_values[:block_rows], up_values[block_rows:]),
        )
        other_pair = (
            jnp.where(split_lower_first, up_keys[block_rows:], up_keys[:block_rows]),
            jnp.where(split_lower_first, up_values[block_rows:], up_values[:block_rows]),
        )
        own_pair, other_pair = (own_pair, other_pair)
        parent = swapped((other_pair[0], other_pair[1]), ("seqhi", "seqlo"), height - 1)
        carry_pair = (
            own_pair[0] + parent[0] + returned[height][0],
            own_pair[1] + parent[1] + returned[height][1],
        )
    key_total = key_grad + spread_rows(0.5 * carry_pair[0], 2)
    value_total = value_grad + spread_rows(carry_pair[1], 2)
    return (
        query_total.astype(jnp.bfloat16)[None],
        key_total.astype(jnp.bfloat16)[None],
        value_total.astype(jnp.bfloat16)[None],
        weight_gradient,
    )


def solution(mesh):
    in_specs = (
        P("dp", ("seqhi", "seqlo"), None),
        P("dp", ("seqhi", "seqlo"), None),
        P("dp", ("seqhi", "seqlo"), None),
        P(),
        P(),
        P("dp", ("seqhi", "seqlo"), None),
    )
    out_specs = (
        P("dp", ("seqhi", "seqlo"), None),
        P("dp", ("seqhi", "seqlo"), None),
        P("dp", ("seqhi", "seqlo"), None),
        P("dp", None),
    )
    return jax.shard_map(shards, mesh=mesh, in_specs=in_specs, out_specs=out_specs, check_vma=False)
```

profile of v0, /device:TPU:1, one launch (start us, length us, event | category | flops | bytes accessed | tf_op | source)
XLA Modules:
  0.0 210.4 jit_solution(2963989376022502578)
XLA Ops:
  7.2 1.2 reshape.433
  8.5 0.3 fusion.63
  9.1 0.3 fusion.59
  9.5 0.5 collective-permute-start.3
  10.2 0.8 copy.316
  11.4 0.3 fusion.60
  12.0 0.4 convert_reduce_fusion.1
  12.9 0.4 fusion.67
  13.5 0.7 convert_element_type.251
  14.5 0.3 fusion.58
  14.9 0.7 fusion.37
  15.5 2.3 %collective-permute-start.4 = (bf16[128,384]{1,0:T(8,128)(2,1)}, bf16[128,384]{1,0:T(8,128)(2,1)S(1)}, u32[]{:S(2)}, u32[]{:S(2)}) collective-permute-start(bf16[128,384]{1,0:T(8,128)(2,1)} %fusion.37), channel_id=1, source_target_pairs={{0,2},{1,3},{2,0},{3,1},{4,6},{5,7},{6,4},{7,5},{8,10},{9,11},{10,... | collective-permute-start | bytes 294920 | tf_op jit(solution)/shard_map/ppermute | solution.py:10
  18.4 0.7 fusion.34
  20.0 0.8 collective-permute-done.4
  20.8 1.0 broadcast_select_fusion.1
  22.3 0.6 copy.454
  22.9 1.1 collective-permute-start.5
  24.0 1.0 broadcast_select_fusion.3
  25.6 0.4 collective-permute-start.2
  26.1 1.0 copy.302
  27.1 0.3 fusion.65
  27.4 1.0 copy.325
  28.6 0.8 copy.328
  30.7 1.9 divide_convert_fusion
  32.6 0.8 copy.388
  33.4 0.9 copy.317
  34.3 1.0 reshape.442
  35.3 1.0 copy.326
  37.1 0.9 broadcast_in_dim.46
  38.0 1.5 reshape.410
  39.5 1.0 copy.330
  40.5 1.1 copy.315
  41.7 1.1 fusion.16
  42.8 1.0 fusion.57
  43.7 0.8 copy.335
  44.6 0.4 multiply_convert_fusion
  45.0 0.4 fusion.70
  45.9 0.3 div.50.clone
  46.2 1.4 div.55
  47.6 1.6 divide_reduce_fusion
  49.7 0.6 convert_element_type.281
  52.8 0.9 fusion.68
  53.8 0.9 copy.390
  54.7 0.8 fusion.44
  56.7 2.1 %fusion.30 = f32[384,384]{1,0:T(8,128)} fusion(bf16[256,384]{0,1:T(8,128)(2,1)} %bitcast.190, bf16[1,256,384]{2,1,0:T(8,128)(2,1)} %param.11), kind=kOutput, calls=%fused_computation.59 | convolution fusion | flops 75497472 | bytes 983040 | tf_op jit(solution)/shard_map/dot_general | solution.py:152
  59.0 0.8 copy.357
  60.1 0.8 copy.349
  62.3 2.4 %collective-permute-start.8 = (f32[128,384]{1,0:T(8,128)S(1)}, f32[128,384]{1,0:T(8,128)}, u32[]{:S(2)}, u32[]{:S(2)}) collective-permute-start(f32[128,384]{1,0:T(8,128)S(1)} %copy.351), channel_id=1, source_target_pairs={{0,2},{1,3},{2,0},{3,1},{4,6},{5,7},{6,4},{7,5},{8,10},{9,11},{10,... | collective-permute-start | bytes 589832 | tf_op jit(solution)/shard_map/ppermute | solution.py:10
  64.7 2.4 %collective-permute-start.10 = (f32[128,384]{1,0:T(8,128)S(1)}, f32[128,384]{1,0:T(8,128)}, u32[]{:S(2)}, u32[]{:S(2)}) collective-permute-start(f32[128,384]{1,0:T(8,128)S(1)} %copy.353), channel_id=1, source_target_pairs={{0,1},{1,0},{2,3},{3,2},{4,5},{5,4},{6,7},{7,6},{8,9},{9,8},{10,11... | collective-permute-start | bytes 589832 | tf_op jit(solution)/shard_map/ppermute | solution.py:10
  67.0 0.5 collective-permute-start.6
  67.5 0.7 add_convert_fusion.2
  68.2 5.9 %collective-permute-done.6 = f32[128,384]{1,0:T(8,128)S(1)} collective-permute-done((f32[128,384]{1,0:T(8,128)}, f32[128,384]{1,0:T(8,128)S(1)}, u32[]{:S(2)}, u32[]{:S(2)}) %collective-permute-start.6) | collective-permute-done | bytes 196640 | tf_op jit(solution)/shard_map/ppermute | solution.py:10
  74.4 5.4 %collective-permute-done.11 = f32[128,384]{1,0:T(8,128)S(1)} collective-permute-done((f32[128,384]{1,0:T(8,128)S(1)}, f32[128,384]{1,0:T(8,128)S(1)}, u32[]{:S(2)}, u32[]{:S(2)}) %collective-permute-start.11) | collective-permute-done | bytes 196640 | tf_op jit(solution)/shard_map/ppermute | solution.py:10
  80.5 109.2 %all-reduce.2.cloned.1.call-done = f32[384,384]{1,0:T(8,128)} async-done(((f32[384,384]{1,0:T(8,128)}), f32[384,384]{1,0:T(8,128)}) %all-reduce.2.cloned.1.call-update) | async-done | bytes 589840 | tf_op jit(solution)/shard_map/psum | solution.py:155
  189.7 1.6 constant_dynamic-slice_fusion
  191.3 1.1 collective-permute-start.12
  192.4 1.0 add_multiply_fusion.1
  193.8 0.6 collective-permute-start.9
  194.4 3.2 %collective-permute-done.12 = f32[128,384]{1,0:T(8,128)} collective-permute-done((f32[128,384]{1,0:T(8,128)S(1)}, f32[128,384]{1,0:T(8,128)}, u32[]{:S(2)}, u32[]{:S(2)}) %collective-permute-start.12) | collective-permute-done | bytes 196640 | tf_op jit(solution)/shard_map/ppermute | solution.py:10
  197.6 1.1 add_add_fusion.1
  199.2 1.1 collective-permute-start.14
  200.3 1.0 add_multiply_fusion
  202.2 0.7 add_convert_fusion.1
  202.9 0.7 add_convert_fusion
  (238 shorter events, 15.4 us)
Async XLA Ops:
  7.2 23.5 %copy-start = (bf16[384,384]{1,0:T(8,128)(2,1)S(1)}, bf16[384,384]{1,0:T(8,128)(2,1)}, u32[]{:S(2)}) copy-start(bf16[384,384]{1,0:T(8,128)(2,1)} %param.10) | copy-start | bytes 884740
  7.2 1.8 copy-start.29
  7.2 182.5 %all-reduce.2.cloned.1.call-start = ((), (), s32[]{:S(2)}) async-start(), calls=%async_computation | async-start | bytes 1179648 | tf_op jit(solution)/shard_map/psum | solution.py:155
  8.4 1.6 copy-start.28
  8.8 2.2 %copy-start.30 = (bf16[1,256,384]{2,1,0:T(8,128)(2,1)S(1)}, bf16[1,256,384]{2,1,0:T(8,128)(2,1)}, u32[]{:S(2)}) copy-start(bf16[1,256,384]{2,1,0:T(8,128)(2,1)} %param.6) | copy-start | bytes 589828
  8.8 5.4 %collective-permute-start = (bf16[128,384]{1,0:T(8,128)(2,1)S(1)}, bf16[128,384]{1,0:T(8,128)(2,1)S(1)}, u32[]{:S(2)}, u32[]{:S(2)}) collective-permute-start(bf16[128,384]{1,0:T(8,128)(2,1)S(1)} %fusion.33), channel_id=1, source_target_pairs={{0,1},{1,0},{2,3},{3,2},{4,5},{5,4},{6,7},{7,6},{8,9},{9,8},{10,11... | collective-permute-start | bytes 294920 | tf_op jit(solution)/shard_map/ppermute | solution.py:10
  9.5 4.7 %collective-permute-start.3 = (bf16[128,384]{1,0:T(8,128)(2,1)S(1)}, bf16[128,384]{1,0:T(8,128)(2,1)S(1)}, u32[]{:S(2)}, u32[]{:S(2)}) collective-permute-start(bf16[128,384]{1,0:T(8,128)(2,1)S(1)} %fusion.36), channel_id=1, source_target_pairs={{0,1},{1,0},{2,3},{3,2},{4,5},{5,4},{6,7},{7,6},{8,9},{9,8},{10,11... | collective-permute-start | bytes 294920 | tf_op jit(solution)/shard_map/ppermute | solution.py:10
  10.2 2.7 %copy-start.1 = (bf16[1,256,384]{1,2,0:T(8,128)(2,1)}, bf16[1,256,384]{1,2,0:T(8,128)(2,1)S(1)}, u32[]{:S(2)}) copy-start(bf16[1,256,384]{1,2,0:T(8,128)(2,1)S(1)} %copy.293) | copy-start | bytes 589828
  10.2 1.8 copy-start.42
  11.2 1.7 copy-start.3
  11.8 7.4 %copy-start.22 = (bf16[128,1,384]{0,2,1:T(8,128)(2,1)}, bf16[128,1,384]{0,2,1:T(8,128)(2,1)S(1)}, u32[]{:S(2)}) copy-start(bf16[128,1,384]{0,2,1:T(8,128)(2,1)S(1)} %copy.296) | copy-start | bytes 294916
  12.0 17.5 %copy-start.40 = (f32[6]{0:T(128)}, f32[6]{0:T(128)S(1)}, u32[]{:S(2)}) copy-start(f32[6]{0:T(128)S(1)} %broadcast_multiply_fusion.1) | copy-start | bytes 76
  12.5 14.6 %copy-start.12 = (bf16[64,384]{0,1:T(8,128)(2,1)}, bf16[64,384]{0,1:T(8,128)(2,1)S(1)}, u32[]{:S(2)}) copy-start(bf16[64,384]{0,1:T(8,128)(2,1)S(1)} %copy.389) | copy-start | bytes 147460
  15.5 5.3 %collective-permute-start.4 = (bf16[128,384]{1,0:T(8,128)(2,1)}, bf16[128,384]{1,0:T(8,128)(2,1)S(1)}, u32[]{:S(2)}, u32[]{:S(2)}) collective-permute-start(bf16[128,384]{1,0:T(8,128)(2,1)} %fusion.37), channel_id=1, source_target_pairs={{0,2},{1,3},{2,0},{3,1},{4,6},{5,7},{6,4},{7,5},{8,10},{9,11},{10,... | collective-permute-start | bytes 294920 | tf_op jit(solution)/shard_map/ppermute | solution.py:10
  19.1 5.0 %collective-permute-start.1 = (bf16[128,384]{1,0:T(8,128)(2,1)}, bf16[128,384]{1,0:T(8,128)(2,1)}, u32[]{:S(2)}, u32[]{:S(2)}) collective-permute-start(bf16[128,384]{1,0:T(8,128)(2,1)} %fusion.34), channel_id=1, source_target_pairs={{0,2},{1,3},{2,0},{3,1},{4,6},{5,7},{6,4},{7,5},{8,10},{9,11},{10,... | collective-permute-start | bytes 294920 | tf_op jit(solution)/shard_map/ppermute | solution.py:10
  19.2 2.6 %copy-start.24 = (bf16[128,384]{0,1:T(8,128)(2,1)}, bf16[128,384]{0,1:T(8,128)(2,1)S(1)}, u32[]{:S(2)}) copy-start(bf16[128,384]{0,1:T(8,128)(2,1)S(1)} %copy.299) | copy-start | bytes 294916
  19.6 2.1 %copy-start.26 = (bf16[128,384]{0,1:T(8,128)(2,1)}, bf16[128,384]{0,1:T(8,128)(2,1)S(1)}, u32[]{:S(2)}) copy-start(bf16[128,384]{0,1:T(8,128)(2,1)S(1)} %copy.321) | copy-start | bytes 294916
  20.8 1.0 copy-start.37
  22.9 12.4 %collective-permute-start.5 = (bf16[128,384]{1,0:T(8,128)(2,1)}, bf16[128,384]{1,0:T(8,128)(2,1)}, u32[]{:S(2)}, u32[]{:S(2)}) collective-permute-start(bf16[128,384]{1,0:T(8,128)(2,1)} %bitcast.146), channel_id=1, source_target_pairs={{0,4},{1,5},{2,6},{3,7},{4,0},{5,1},{6,2},{7,3},{8,12},{9,13},{10,... | collective-permute-start | bytes 294920 | tf_op jit(solution)/shard_map/ppermute | solution.py:10
  25.3 4.3 %copy-start.35 = (bf16[32,6,64]{2,1,0:T(8,128)(2,1)S(1)}, bf16[32,6,64]{2,1,0:T(8,128)(2,1)}, u32[]{:S(2)}) copy-start(bf16[32,6,64]{2,1,0:T(8,128)(2,1)} %convert_element_type.251) | copy-start | bytes 73732
  25.6 3.8 %collective-permute-start.2 = (bf16[128,384]{1,0:T(8,128)(2,1)S(1)}, bf16[128,384]{1,0:T(8,128)(2,1)S(1)}, u32[]{:S(2)}, u32[]{:S(2)}) collective-permute-start(bf16[128,384]{1,0:T(8,128)(2,1)S(1)} %fusion.35), channel_id=1, source_target_pairs={{0,4},{1,5},{2,6},{3,7},{4,0},{5,1},{6,2},{7,3},{8,12},{9,13},{10,... | collective-permute-start | bytes 294920 | tf_op jit(solution)/shard_map/ppermute | solution.py:10
  27.1 3.4 %copy-start.14 = (bf16[128,384]{0,1:T(8,128)(2,1)}, bf16[128,384]{0,1:T(8,128)(2,1)S(1)}, u32[]{:S(2)}) copy-start(bf16[128,384]{0,1:T(8,128)(2,1)S(1)} %copy.302) | copy-start | bytes 294916
  28.4 0.9 copy-start.20
  29.5 1.0 copy-start.16
  29.8 6.5 %copy-start.7 = (f32[6,32,128]{2,1,0:T(8,128)}, f32[6,32,128]{2,1,0:T(8,128)S(1)}, u32[]{:S(2)}) copy-start(f32[6,32,128]{2,1,0:T(8,128)S(1)} %get-tuple-element.37) | copy-start | bytes 294916
  32.6 4.2 %copy-start.38 = (f32[64,384]{1,0:T(8,128)S(1)}, f32[64,384]{1,0:T(8,128)}, u32[]{:S(2)}) copy-start(f32[64,384]{1,0:T(8,128)} %copy.328) | copy-start | bytes 294916
  36.3 0.7 copy-start.18
  40.5 2.3 %copy-start.5 = (bf16[1,256,384]{1,2,0:T(8,128)(2,1)S(1)}, bf16[1,256,384]{1,2,0:T(8,128)(2,1)}, u32[]{:S(2)}) copy-start(bf16[1,256,384]{1,2,0:T(8,128)(2,1)} %copy.316) | copy-start | bytes 589828
  40.5 2.3 %copy-start.10 = (f32[256,384]{0,1:T(8,128)S(1)}, f32[256,384]{0,1:T(8,128)}, u32[]{:S(2)}) copy-start(f32[256,384]{0,1:T(8,128)} %copy.317) | copy-start | bytes 1179652
  41.6 1.1 copy-start.11
  42.8 1.8 copy-start.41
  43.7 1.2 copy-start.4
  44.6 1.0 copy-start.2
  45.0 0.9 copy-start.33
  45.9 1.7 copy-start.6
  47.6 2.7 %copy-start.34 = (f32[256,6]{1,0:T(8,128)S(1)}, f32[256,6]{1,0:T(8,128)}, u32[]{:S(2)}) copy-start(f32[256,6]{1,0:T(8,128)} %copy.335) | copy-start | bytes 18436
  47.6 3.4 %copy-start.8 = (f32[6,32,128]{2,1,0:T(8,128)S(1)}, f32[6,32,128]{2,1,0:T(8,128)}, u32[]{:S(2)}) copy-start(f32[6,32,128]{2,1,0:T(8,128)} %copy-done.7) | copy-start | bytes 294916
  47.6 3.7 %copy-start.19 = (bf16[128,384]{0,1:T(8,128)(2,1)S(1)}, bf16[128,384]{0,1:T(8,128)(2,1)}, u32[]{:S(2)}) copy-start(bf16[128,384]{0,1:T(8,128)(2,1)} %copy-done.18) | copy-start | bytes 294916
  49.3 2.2 %copy-start.17 = (bf16[128,384]{0,1:T(8,128)(2,1)S(1)}, bf16[128,384]{0,1:T(8,128)(2,1)}, u32[]{:S(2)}) copy-start(bf16[128,384]{0,1:T(8,128)(2,1)} %copy-done.16) | copy-start | bytes 294916
  49.3 2.3 %copy-start.36 = (bf16[32,6,64]{2,1,0:T(8,128)(2,1)S(1)}, bf16[32,6,64]{2,1,0:T(8,128)(2,1)}, u32[]{:S(2)}) copy-start(bf16[32,6,64]{2,1,0:T(8,128)(2,1)} %convert_element_type.251) | copy-start | bytes 73732
  50.3 2.0 copy-start.27
  50.8 1.8 copy-start.23
  51.3 1.6 copy-start.25
  52.0 3.5 %copy-start.21 = (bf16[128,384]{0,1:T(8,128)(2,1)S(1)}, bf16[128,384]{0,1:T(8,128)(2,1)}, u32[]{:S(2)}) copy-start(bf16[128,384]{0,1:T(8,128)(2,1)} %copy-done.20) | copy-start | bytes 294916
  52.3 3.5 %copy-start.13 = (bf16[64,384]{0,1:T(8,128)(2,1)S(1)}, bf16[64,384]{0,1:T(8,128)(2,1)}, u32[]{:S(2)}) copy-start(bf16[64,384]{0,1:T(8,128)(2,1)} %copy-done.12) | copy-start | bytes 147460
  52.3 3.7 %copy-start.15 = (bf16[128,384]{0,1:T(8,128)(2,1)S(1)}, bf16[128,384]{0,1:T(8,128)(2,1)}, u32[]{:S(2)}) copy-start(bf16[128,384]{0,1:T(8,128)(2,1)} %copy-done.14) | copy-start | bytes 294916
  52.6 3.6 %copy-start.9 = (f32[6,64,256]{2,1,0:T(8,128)S(1)}, f32[6,64,256]{2,1,0:T(8,128)}, u32[]{:S(2)}) copy-start(f32[6,64,256]{2,1,0:T(8,128)} %fusion.16) | copy-start | bytes 1179652
  56.5 3.4 %copy-start.32 = (f32[6,64,128]{2,1,0:T(8,128)S(1)}, f32[6,64,128]{2,1,0:T(8,128)}, u32[]{:S(2)}) copy-start(f32[6,64,128]{2,1,0:T(8,128)} %fusion.44) | copy-start | bytes 589828
  58.8 2.2 %copy-start.31 = (f32[6,64,128]{2,1,0:T(8,128)S(1)}, f32[6,64,128]{2,1,0:T(8,128)}, u32[]{:S(2)}) copy-start(f32[6,64,128]{2,1,0:T(8,128)} %fusion.68) | copy-start | bytes 589828
  61.6 12.5 %copy-start.39 = (f32[128,384]{1,0:T(8,128)S(1)}, f32[128,384]{1,0:T(8,128)}, u32[]{:S(2)}) copy-start(f32[128,384]{1,0:T(8,128)} %copy.357) | copy-start | bytes 589828
  62.3 129.0 %collective-permute-start.8 = (f32[128,384]{1,0:T(8,128)S(1)}, f32[128,384]{1,0:T(8,128)}, u32[]{:S(2)}, u32[]{:S(2)}) collective-permute-start(f32[128,384]{1,0:T(8,128)S(1)} %copy.351), channel_id=1, source_target_pairs={{0,2},{1,3},{2,0},{3,1},{4,6},{5,7},{6,4},{7,5},{8,10},{9,11},{10,... | collective-permute-start | bytes 589832 | tf_op jit(solution)/shard_map/ppermute | solution.py:10
  64.7 135.6 %collective-permute-start.10 = (f32[128,384]{1,0:T(8,128)S(1)}, f32[128,384]{1,0:T(8,128)}, u32[]{:S(2)}, u32[]{:S(2)}) collective-permute-start(f32[128,384]{1,0:T(8,128)S(1)} %copy.353), channel_id=1, source_target_pairs={{0,1},{1,0},{2,3},{3,2},{4,5},{5,4},{6,7},{7,6},{8,9},{9,8},{10,11... | collective-permute-start | bytes 589832 | tf_op jit(solution)/shard_map/ppermute | solution.py:10
  67.0 134.6 %collective-permute-start.15 = (f32[128,384]{1,0:T(8,128)S(1)}, f32[128,384]{1,0:T(8,128)S(1)}, u32[]{:S(2)}, u32[]{:S(2)}) collective-permute-start(f32[128,384]{1,0:T(8,128)S(1)} %copy.361), channel_id=1, source_target_pairs={{0,1},{1,0},{2,3},{3,2},{4,5},{5,4},{6,7},{7,6},{8,9},{9,8},{10,11... | collective-permute-start | bytes 589832 | tf_op jit(solution)/shard_map/ppermute | solution.py:10
  67.0 7.1 %collective-permute-start.6 = (f32[128,384]{1,0:T(8,128)}, f32[128,384]{1,0:T(8,128)S(1)}, u32[]{:S(2)}, u32[]{:S(2)}) collective-permute-start(f32[128,384]{1,0:T(8,128)} %copy.349), channel_id=1, source_target_pairs={{0,4},{1,5},{2,6},{3,7},{4,0},{5,1},{6,2},{7,3},{8,12},{9,13},{10,... | collective-permute-start | bytes 589832 | tf_op jit(solution)/shard_map/ppermute | solution.py:10
  67.5 126.9 %collective-permute-start.13 = (f32[128,384]{1,0:T(8,128)S(1)}, f32[128,384]{1,0:T(8,128)}, u32[]{:S(2)}, u32[]{:S(2)}) collective-permute-start(f32[128,384]{1,0:T(8,128)S(1)} %copy.359), channel_id=1, source_target_pairs={{0,2},{1,3},{2,0},{3,1},{4,6},{5,7},{6,4},{7,5},{8,10},{9,11},{10,... | collective-permute-start | bytes 589832 | tf_op jit(solution)/shard_map/ppermute | solution.py:10
  74.1 5.6 %collective-permute-start.11 = (f32[128,384]{1,0:T(8,128)S(1)}, f32[128,384]{1,0:T(8,128)S(1)}, u32[]{:S(2)}, u32[]{:S(2)}) collective-permute-start(f32[128,384]{1,0:T(8,128)S(1)} %copy-done.39), channel_id=1, source_target_pairs={{0,4},{1,5},{2,6},{3,7},{4,0},{5,1},{6,2},{7,3},{8,12},{9,13},{10,... | collective-permute-start | bytes 589832 | tf_op jit(solution)/shard_map/ppermute | solution.py:10
  79.8 112.6 %collective-permute-start.7 = (f32[128,384]{1,0:T(8,128)S(1)}, f32[128,384]{1,0:T(8,128)S(1)}, u32[]{:S(2)}, u32[]{:S(2)}) collective-permute-start(f32[128,384]{1,0:T(8,128)S(1)} %select_n.151), channel_id=1, source_target_pairs={{0,2},{1,3},{2,0},{3,1},{4,6},{5,7},{6,4},{7,5},{8,10},{9,11},{10,... | collective-permute-start | bytes 589832 | tf_op jit(solution)/shard_map/ppermute | solution.py:10
  191.3 6.4 %collective-permute-start.12 = (f32[128,384]{1,0:T(8,128)S(1)}, f32[128,384]{1,0:T(8,128)}, u32[]{:S(2)}, u32[]{:S(2)}) collective-permute-start(f32[128,384]{1,0:T(8,128)S(1)} %select_n.159), channel_id=1, source_target_pairs={{0,2},{1,3},{2,0},{3,1},{4,6},{5,7},{6,4},{7,5},{8,10},{9,11},{10,... | collective-permute-start | bytes 589832 | tf_op jit(solution)/shard_map/ppermute | solution.py:10
  193.8 6.4 %collective-permute-start.9 = (f32[128,384]{1,0:T(8,128)S(1)}, f32[128,384]{1,0:T(8,128)S(1)}, u32[]{:S(2)}, u32[]{:S(2)}) collective-permute-start(f32[128,384]{1,0:T(8,128)S(1)} %select_n.155), channel_id=1, source_target_pairs={{0,1},{1,0},{2,3},{3,2},{4,5},{5,4},{6,7},{7,6},{8,9},{9,8},{10,11... | collective-permute-start | bytes 589832 | tf_op jit(solution)/shard_map/ppermute | solution.py:10
  199.2 2.5 %collective-permute-start.14 = (f32[128,384]{1,0:T(8,128)S(1)}, f32[128,384]{1,0:T(8,128)S(1)}, u32[]{:S(2)}, u32[]{:S(2)}) collective-permute-start(f32[128,384]{1,0:T(8,128)S(1)} %select_n.163), channel_id=1, source_target_pairs={{0,1},{1,0},{2,3},{3,2},{4,5},{5,4},{6,7},{7,6},{8,9},{9,8},{10,11... | collective-permute-start | bytes 589832 | tf_op jit(solution)/shard_map/ppermute | solution.py:10
Sparse Core Ops, SparseCore 0:
  59.0 130.6 all-reduce.1
where the time goes:
time: 211 us; the launch traced here: 210 us
  waiting for transfers between devices  125 us (59%)
  local copies, waits for them, and re-layouts  32.4 us (15%)
  between operations  15.4 us (7%)
  other arithmetic  12.8 us (6%)
  starting transfers between devices  12.6 us (6%)
  matrix products  12.6 us (6%)
    psum x1, waiting for transfers between devices, shards(): summed = lax.psum(weight_term, ('dp', 'seqhi', 'seqlo'))  109 us
    ppermute x16, waiting for transfers between devices, swapped(): return lax.ppermute(value, axis, pairs)  15.3 us
    ppermute x16, starting transfers between devices, swapped(): return lax.ppermute(value, axis, pairs)  12.6 us
  transfers between devices with their start and end apart: 17, of which 5 were waited for; matrix products, arithmetic and copies ran while one was open for 14% of the time, Pallas kernels for 0%

commit v1 on v0

--- a/solution.py
+++ b/solution.py
@@ -152,7 +152,7 @@
     weight_term = lax.dot_general(
         attended, cotan_local, (((0,), (0,)), ((), ())), preferred_element_type=jnp.float32
     )
-    summed = lax.psum(weight_term, ("dp", "seqhi", "seqlo"))
+    summed = lax.psum(lax.psum(weight_term, ("seqhi", "seqlo")), "dp")
     weight_gradient = lax.dynamic_slice_in_dim(summed, lax.axis_index("dp") * own_rows, own_rows, 0)
     backward = lax.dot_general(
         cotan_local, out_weight, (((1,), (1,)), ((), ())), preferred_element_type=jnp.float32

time: 211 us -> 168 us (0.80)
  waiting for transfers between devices: 125 us -> 78.2 us
  starting transfers between devices: 12.6 us -> 15.3 us
    psum x1 -> x2, waiting for transfers between devices: 109 us -> 64.6 us  [shards(): summed = lax.psum(lax.psum(weight_term, ('seqhi', 'seqlo')), 'dp')]
    ppermute x16, starting transfers between devices: 12.6 us -> 15.2 us  [swapped(): return lax.ppermute(value, axis, pairs)]
  transfers between devices with their start and end apart: 17 -> 18, of which waited for: 5 -> 7; matrix products, arithmetic and copies ran while one was open for 14% -> 18% of each run, Pallas kernels for 0% -> 0%
where the time goes in v1:
time: 168 us; the launch traced here: 167 us
  waiting for transfers between devices  78.2 us (47%)
  local copies, waits for them, and re-layouts  32.4 us (19%)
  between operations  15.4 us (9%)
  starting transfers between devices  15.3 us (9%)
  other arithmetic  12.8 us (8%)
  matrix products  12.6 us (8%)
    psum x2, waiting for transfers between devices, shards(): summed = lax.psum(lax.psum(weight_term, ('seqhi', 'seqlo')), 'dp')  64.6 us
    ppermute x16, starting transfers between devices, swapped(): return lax.ppermute(value, axis, pairs)  15.2 us
    ppermute x16, waiting for transfers between devices, swapped(): return lax.ppermute(value, axis, pairs)  13.6 us
    reshape x12, local copies, waits for them, and re-layouts, spread_rows(): return widened.reshape((matrix.shape[0] * factor,) + matrix.shape[1:])  3.99 us
    ppermute x6, local copies, waits for them, and re-layouts, swapped(): return lax.ppermute(value, axis, pairs)  3.39 us
  transfers between devices with their start and end apart: 18, of which 7 were waited for; matrix products, arithmetic and copies ran while one was open for 18% of the time, Pallas kernels for 0%

profile of v1, /device:TPU:1, one launch (start us, length us, event | category | flops | bytes accessed | tf_op | source)
XLA Modules:
  0.0 166.8 jit_solution(9592152932415819783)
XLA Ops:
  7.2 1.2 reshape.433
  8.5 0.3 fusion.63
  9.1 0.3 fusion.59
  9.5 0.5 collective-permute-start.3
  10.2 0.8 copy.316
  11.4 0.3 fusion.60
  12.0 0.4 convert_reduce_fusion.1
  12.9 0.4 fusion.67
  13.5 0.7 convert_element_type.251
  14.9 0.7 fusion.37
  15.5 2.3 %collective-permute-start.4 = (bf16[128,384]{1,0:T(8,128)(2,1)}, bf16[128,384]{1,0:T(8,128)(2,1)S(1)}, u32[]{:S(2)}, u32[]{:S(2)}) collective-permute-start(bf16[128,384]{1,0:T(8,128)(2,1)} %fusion.37), channel_id=1, source_target_pairs={{0,2},{1,3},{2,0},{3,1},{4,6},{5,7},{6,4},{7,5},{8,10},{9,11},{10,... | collective-permute-start | bytes 294920 | tf_op jit(solution)/shard_map/ppermute | solution.py:10
  18.4 0.7 fusion.34
  20.0 0.8 collective-permute-done.4
  20.8 1.0 broadcast_select_fusion.1
  22.3 0.6 copy.454
  22.9 1.1 collective-permute-start.5
  24.0 1.0 broadcast_select_fusion.3
  25.6 0.4 collective-permute-start.2
  26.1 1.0 copy.302
  27.1 0.3 fusion.65
  27.4 1.0 copy.325
  28.6 0.8 copy.328
  30.7 1.9 %divide_convert_fusion = (bf16[256,384]{1,0:T(8,128)(2,1)}, f32[256,384]{1,0:T(8,128)S(1)}) fusion(f32[256,384]{1,0:T(8,128)S(1)} %copy.314, bf16[384,384]{1,0:T(8,128)(2,1)S(1)} %copy-done, bf16[1,256,384]{2,1,0:T(8,128)(2,1)} %param.11), kind=kOutput, calls=%fused_computation.35 | convolution fusion | flops 75890688 | bytes 1474560 | tf_op jit(solution)/shard_map/dot_general | solution.py:157
  32.6 0.8 copy.388
  33.4 0.9 copy.317
  34.3 1.0 reshape.442
  35.3 1.0 copy.326
  37.1 0.9 broadcast_in_dim.46
  38.0 1.5 reshape.410
  39.5 1.0 copy.330
  40.5 1.1 copy.315
  41.7 1.1 fusion.16
  42.8 1.0 fusion.57
  43.7 0.8 copy.335
  44.6 0.4 multiply_convert_fusion
  45.0 0.4 fusion.70
  45.9 0.3 div.50.clone
  46.2 1.4 div.55
  47.6 1.6 divide_reduce_fusion
  49.7 0.6 convert_element_type.281
  52.8 0.9 fusion.68
  53.8 0.9 copy.390
  54.7 0.8 fusion.44
  56.7 2.1 %fusion.30 = f32[384,384]{1,0:T(8,128)} fusion(bf16[256,384]{0,1:T(8,128)(2,1)} %bitcast.190, bf16[1,256,384]{2,1,0:T(8,128)(2,1)} %param.11), kind=kOutput, calls=%fused_computation.59 | convolution fusion | flops 75497472 | bytes 983040 | tf_op jit(solution)/shard_map/dot_general | solution.py:152
  59.1 0.8 copy.357
  60.1 0.8 copy.349
  62.3 2.4 %collective-permute-start.8 = (f32[128,384]{1,0:T(8,128)S(1)}, f32[128,384]{1,0:T(8,128)}, u32[]{:S(2)}, u32[]{:S(2)}) collective-permute-start(f32[128,384]{1,0:T(8,128)S(1)} %copy.351), channel_id=1, source_target_pairs={{0,2},{1,3},{2,0},{3,1},{4,6},{5,7},{6,4},{7,5},{8,10},{9,11},{10,... | collective-permute-start | bytes 589832 | tf_op jit(solution)/shard_map/ppermute | solution.py:10
  64.7 2.4 %collective-permute-start.10 = (f32[128,384]{1,0:T(8,128)S(1)}, f32[128,384]{1,0:T(8,128)}, u32[]{:S(2)}, u32[]{:S(2)}) collective-permute-start(f32[128,384]{1,0:T(8,128)S(1)} %copy.353), channel_id=1, source_target_pairs={{0,1},{1,0},{2,3},{3,2},{4,5},{5,4},{6,7},{7,6},{8,9},{9,8},{10,11... | collective-permute-start | bytes 589832 | tf_op jit(solution)/shard_map/ppermute | solution.py:10
  67.1 0.5 collective-permute-start.6
  67.6 0.7 add_convert_fusion.2
  68.3 7.0 %collective-permute-done.6 = f32[128,384]{1,0:T(8,128)S(1)} collective-permute-done((f32[128,384]{1,0:T(8,128)}, f32[128,384]{1,0:T(8,128)S(1)}, u32[]{:S(2)}, u32[]{:S(2)}) %collective-permute-start.6) | collective-permute-done | bytes 196640 | tf_op jit(solution)/shard_map/ppermute | solution.py:10
  75.7 5.1 %collective-permute-done.11 = f32[128,384]{1,0:T(8,128)S(1)} collective-permute-done((f32[128,384]{1,0:T(8,128)S(1)}, f32[128,384]{1,0:T(8,128)S(1)}, u32[]{:S(2)}, u32[]{:S(2)}) %collective-permute-start.11) | collective-permute-done | bytes 196640 | tf_op jit(solution)/shard_map/ppermute | solution.py:10
  81.3 35.5 %all-reduce.3.cloned.1.call-done = f32[384,384]{1,0:T(8,128)} async-done(((f32[384,384]{1,0:T(8,128)}), f32[384,384]{1,0:T(8,128)}) %all-reduce.3.cloned.1.call-update) | async-done | bytes 589840 | tf_op jit(solution)/shard_map/psum | solution.py:155
  116.8 0.5 collective-permute-start.12
  117.3 1.0 add_multiply_fusion.1
  118.7 2.1 %collective-permute-start.9 = (f32[128,384]{1,0:T(8,128)S(1)}, f32[128,384]{1,0:T(8,128)S(1)}, u32[]{:S(2)}, u32[]{:S(2)}) collective-permute-start(f32[128,384]{1,0:T(8,128)S(1)} %select_n.155), channel_id=1, source_target_pairs={{0,1},{1,0},{2,3},{3,2},{4,5},{5,4},{6,7},{7,6},{8,9},{9,8},{10,11... | collective-permute-start | bytes 589832 | tf_op jit(solution)/shard_map/ppermute | solution.py:10
  120.8 0.7 collective-permute-done.12
  121.5 1.1 add_add_fusion.1
  123.0 2.9 %collective-permute-start.14 = (f32[128,384]{1,0:T(8,128)S(1)}, f32[128,384]{1,0:T(8,128)S(1)}, u32[]{:S(2)}, u32[]{:S(2)}) collective-permute-start(f32[128,384]{1,0:T(8,128)S(1)} %select_n.163), channel_id=1, source_target_pairs={{0,1},{1,0},{2,3},{3,2},{4,5},{5,4},{6,7},{7,6},{8,9},{9,8},{10,11... | collective-permute-start | bytes 589832 | tf_op jit(solution)/shard_map/ppermute | solution.py:10
  125.9 1.0 add_multiply_fusion
  127.9 0.7 add_convert_fusion.1
  128.6 0.7 add_convert_fusion
  129.3 29.1 %all-reduce.5.cloned.1.call-done = f32[384,384]{1,0:T(8,128)} async-done(((f32[384,384]{1,0:T(8,128)}), f32[384,384]{1,0:T(8,128)}) %all-reduce.5.cloned.1.call-update) | async-done | bytes 589840 | tf_op jit(solution)/shard_map/psum | solution.py:155
  158.4 1.6 constant_dynamic-slice_fusion
  (241 shorter events, 15.8 us)
Async XLA Ops:
  7.2 23.5 %copy-start = (bf16[384,384]{1,0:T(8,128)(2,1)S(1)}, bf16[384,384]{1,0:T(8,128)(2,1)}, u32[]{:S(2)}) copy-start(bf16[384,384]{1,0:T(8,128)(2,1)} %param.10) | copy-start | bytes 884740
  7.2 1.8 %copy-start.29 = (bf16[1,256,384]{2,1,0:T(8,128)(2,1)S(1)}, bf16[1,256,384]{2,1,0:T(8,128)(2,1)}, u32[]{:S(2)}) copy-start(bf16[1,256,384]{2,1,0:T(8,128)(2,1)} %param.8) | copy-start | bytes 589828
  7.2 109.5 %all-reduce.3.cloned.1.call-start = ((), (), s32[]{:S(2)}) async-start(), calls=%async_computation | async-start | bytes 1179648 | tf_op jit(solution)/shard_map/psum | solution.py:155
  8.4 1.6 copy-start.28
  8.8 2.2 %copy-start.30 = (bf16[1,256,384]{2,1,0:T(8,128)(2,1)S(1)}, bf16[1,256,384]{2,1,0:T(8,128)(2,1)}, u32[]{:S(2)}) copy-start(bf16[1,256,384]{2,1,0:T(8,128)(2,1)} %param.6) | copy-start | bytes 589828
  8.8 5.4 %collective-permute-start = (bf16[128,384]{1,0:T(8,128)(2,1)S(1)}, bf16[128,384]{1,0:T(8,128)(2,1)S(1)}, u32[]{:S(2)}, u32[]{:S(2)}) collective-permute-start(bf16[128,384]{1,0:T(8,128)(2,1)S(1)} %fusion.33), channel_id=1, source_target_pairs={{0,1},{1,0},{2,3},{3,2},{4,5},{5,4},{6,7},{7,6},{8,9},{9,8},{10,11... | collective-permute-start | bytes 294920 | tf_op jit(solution)/shard_map/ppermute | solution.py:10
  9.5 4.7 %collective-permute-start.3 = (bf16[128,384]{1,0:T(8,128)(2,1)S(1)}, bf16[128,384]{1,0:T(8,128)(2,1)S(1)}, u32[]{:S(2)}, u32[]{:S(2)}) collective-permute-start(bf16[128,384]{1,0:T(8,128)(2,1)S(1)} %fusion.36), channel_id=1, source_target_pairs={{0,1},{1,0},{2,3},{3,2},{4,5},{5,4},{6,7},{7,6},{8,9},{9,8},{10,11... | collective-permute-start | bytes 294920 | tf_op jit(solution)/shard_map/ppermute | solution.py:10
  10.2 2.7 %copy-start.1 = (bf16[1,256,384]{1,2,0:T(8,128)(2,1)}, bf16[1,256,384]{1,2,0:T(8,128)(2,1)S(1)}, u32[]{:S(2)}) copy-start(bf16[1,256,384]{1,2,0:T(8,128)(2,1)S(1)} %copy.293) | copy-start | bytes 589828
  10.2 1.8 %copy-start.42 = (f32[6]{0:T(128)S(1)}, f32[6]{0:T(128)}, u32[]{:S(2)}) copy-start(f32[6]{0:T(128)} %param.9) | copy-start | bytes 76
  11.2 1.7 %copy-start.3 = (bf16[1,256,384]{1,2,0:T(8,128)(2,1)}, bf16[1,256,384]{1,2,0:T(8,128)(2,1)S(1)}, u32[]{:S(2)}) copy-start(bf16[1,256,384]{1,2,0:T(8,128)(2,1)S(1)} %copy.292) | copy-start | bytes 589828
  11.8 7.4 %copy-start.22 = (bf16[128,1,384]{0,2,1:T(8,128)(2,1)}, bf16[128,1,384]{0,2,1:T(8,128)(2,1)S(1)}, u32[]{:S(2)}) copy-start(bf16[128,1,384]{0,2,1:T(8,128)(2,1)S(1)} %copy.296) | copy-start | bytes 294916
  12.0 17.5 %copy-start.40 = (f32[6]{0:T(128)}, f32[6]{0:T(128)S(1)}, u32[]{:S(2)}) copy-start(f32[6]{0:T(128)S(1)} %broadcast_multiply_fusion.1) | copy-start | bytes 76
  12.5 14.6 %copy-start.12 = (bf16[64,384]{0,1:T(8,128)(2,1)}, bf16[64,384]{0,1:T(8,128)(2,1)S(1)}, u32[]{:S(2)}) copy-start(bf16[64,384]{0,1:T(8,128)(2,1)S(1)} %copy.389) | copy-start | bytes 147460
  15.5 5.3 %collective-permute-start.4 = (bf16[128,384]{1,0:T(8,128)(2,1)}, bf16[128,384]{1,0:T(8,128)(2,1)S(1)}, u32[]{:S(2)}, u32[]{:S(2)}) collective-permute-start(bf16[128,384]{1,0:T(8,128)(2,1)} %fusion.37), channel_id=1, source_target_pairs={{0,2},{1,3},{2,0},{3,1},{4,6},{5,7},{6,4},{7,5},{8,10},{9,11},{10,... | collective-permute-start | bytes 294920 | tf_op jit(solution)/shard_map/ppermute | solution.py:10
  19.1 5.0 %collective-permute-start.1 = (bf16[128,384]{1,0:T(8,128)(2,1)}, bf16[128,384]{1,0:T(8,128)(2,1)}, u32[]{:S(2)}, u32[]{:S(2)}) collective-permute-start(bf16[128,384]{1,0:T(8,128)(2,1)} %fusion.34), channel_id=1, source_target_pairs={{0,2},{1,3},{2,0},{3,1},{4,6},{5,7},{6,4},{7,5},{8,10},{9,11},{10,... | collective-permute-start | bytes 294920 | tf_op jit(solution)/shard_map/ppermute | solution.py:10
  19.2 2.6 %copy-start.24 = (bf16[128,384]{0,1:T(8,128)(2,1)}, bf16[128,384]{0,1:T(8,128)(2,1)S(1)}, u32[]{:S(2)}) copy-start(bf16[128,384]{0,1:T(8,128)(2,1)S(1)} %copy.299) | copy-start | bytes 294916
  19.6 2.1 %copy-start.26 = (bf16[128,384]{0,1:T(8,128)(2,1)}, bf16[128,384]{0,1:T(8,128)(2,1)S(1)}, u32[]{:S(2)}) copy-start(bf16[128,384]{0,1:T(8,128)(2,1)S(1)} %copy.321) | copy-start | bytes 294916
  20.8 1.0 copy-start.37
  22.9 12.4 %collective-permute-start.5 = (bf16[128,384]{1,0:T(8,128)(2,1)}, bf16[128,384]{1,0:T(8,128)(2,1)}, u32[]{:S(2)}, u32[]{:S(2)}) collective-permute-start(bf16[128,384]{1,0:T(8,128)(2,1)} %bitcast.146), channel_id=1, source_target_pairs={{0,4},{1,5},{2,6},{3,7},{4,0},{5,1},{6,2},{7,3},{8,12},{9,13},{10,... | collective-permute-start | bytes 294920 | tf_op jit(solution)/shard_map/ppermute | solution.py:10
  25.3 4.3 %copy-start.35 = (bf16[32,6,64]{2,1,0:T(8,128)(2,1)S(1)}, bf16[32,6,64]{2,1,0:T(8,128)(2,1)}, u32[]{:S(2)}) copy-start(bf16[32,6,64]{2,1,0:T(8,128)(2,1)} %convert_element_type.251) | copy-start | bytes 73732
  25.6 3.8 %collective-permute-start.2 = (bf16[128,384]{1,0:T(8,128)(2,1)S(1)}, bf16[128,384]{1,0:T(8,128)(2,1)S(1)}, u32[]{:S(2)}, u32[]{:S(2)}) collective-permute-start(bf16[128,384]{1,0:T(8,128)(2,1)S(1)} %fusion.35), channel_id=1, source_target_pairs={{0,4},{1,5},{2,6},{3,7},{4,0},{5,1},{6,2},{7,3},{8,12},{9,13},{10,... | collective-permute-start | bytes 294920 | tf_op jit(solution)/shard_map/ppermute | solution.py:10
  27.1 3.4 %copy-start.14 = (bf16[128,384]{0,1:T(8,128)(2,1)}, bf16[128,384]{0,1:T(8,128)(2,1)S(1)}, u32[]{:S(2)}) copy-start(bf16[128,384]{0,1:T(8,128)(2,1)S(1)} %copy.302) | copy-start | bytes 294916
  28.4 0.9 copy-start.20
  29.5 1.0 copy-start.16
  29.8 6.5 %copy-start.7 = (f32[6,32,128]{2,1,0:T(8,128)}, f32[6,32,128]{2,1,0:T(8,128)S(1)}, u32[]{:S(2)}) copy-start(f32[6,32,128]{2,1,0:T(8,128)S(1)} %get-tuple-element.37) | copy-start | bytes 294916
  32.6 4.2 %copy-start.38 = (f32[64,384]{1,0:T(8,128)S(1)}, f32[64,384]{1,0:T(8,128)}, u32[]{:S(2)}) copy-start(f32[64,384]{1,0:T(8,128)} %copy.328) | copy-start | bytes 294916
  36.3 0.7 copy-start.18
  40.5 2.3 %copy-start.5 = (bf16[1,256,384]{1,2,0:T(8,128)(2,1)S(1)}, bf16[1,256,384]{1,2,0:T(8,128)(2,1)}, u32[]{:S(2)}) copy-start(bf16[1,256,384]{1,2,0:T(8,128)(2,1)} %copy.316) | copy-start | bytes 589828
  40.5 2.3 %copy-start.10 = (f32[256,384]{0,1:T(8,128)S(1)}, f32[256,384]{0,1:T(8,128)}, u32[]{:S(2)}) copy-start(f32[256,384]{0,1:T(8,128)} %copy.317) | copy-start | bytes 1179652
  41.6 1.1 copy-start.11
  42.8 1.8 %copy-start.41 = (f32[6]{0:T(128)S(1)}, f32[6]{0:T(128)}, u32[]{:S(2)}) copy-start(f32[6]{0:T(128)} %copy-done.40) | copy-start | bytes 76
  43.7 1.2 copy-start.4
  44.6 1.0 copy-start.2
  45.0 0.9 copy-start.33
  45.9 1.7 %copy-start.6 = (f32[128,2,384]{2,1,0:T(2,128)S(1)}, f32[128,2,384]{2,1,0:T(2,128)}, u32[]{:S(2)}) copy-start(f32[128,2,384]{2,1,0:T(2,128)} %reshape.442) | copy-start | bytes 1179652
  47.6 2.7 %copy-start.34 = (f32[256,6]{1,0:T(8,128)S(1)}, f32[256,6]{1,0:T(8,128)}, u32[]{:S(2)}) copy-start(f32[256,6]{1,0:T(8,128)} %copy.335) | copy-start | bytes 18436
  47.6 3.4 %copy-start.8 = (f32[6,32,128]{2,1,0:T(8,128)S(1)}, f32[6,32,128]{2,1,0:T(8,128)}, u32[]{:S(2)}) copy-start(f32[6,32,128]{2,1,0:T(8,128)} %copy-done.7) | copy-start | bytes 294916
  47.6 3.7 %copy-start.19 = (bf16[128,384]{0,1:T(8,128)(2,1)S(1)}, bf16[128,384]{0,1:T(8,128)(2,1)}, u32[]{:S(2)}) copy-start(bf16[128,384]{0,1:T(8,128)(2,1)} %copy-done.18) | copy-start | bytes 294916
  49.3 2.2 %copy-start.17 = (bf16[128,384]{0,1:T(8,128)(2,1)S(1)}, bf16[128,384]{0,1:T(8,128)(2,1)}, u32[]{:S(2)}) copy-start(bf16[128,384]{0,1:T(8,128)(2,1)} %copy-done.16) | copy-start | bytes 294916
  49.3 2.3 %copy-start.36 = (bf16[32,6,64]{2,1,0:T(8,128)(2,1)S(1)}, bf16[32,6,64]{2,1,0:T(8,128)(2,1)}, u32[]{:S(2)}) copy-start(bf16[32,6,64]{2,1,0:T(8,128)(2,1)} %convert_element_type.251) | copy-start | bytes 73732
  50.3 2.0 %copy-start.27 = (bf16[128,384]{0,1:T(8,128)(2,1)S(1)}, bf16[128,384]{0,1:T(8,128)(2,1)}, u32[]{:S(2)}) copy-start(bf16[128,384]{0,1:T(8,128)(2,1)} %copy-done.26) | copy-start | bytes 294916
  50.8 1.8 %copy-start.23 = (bf16[128,1,384]{0,2,1:T(8,128)(2,1)S(1)}, bf16[128,1,384]{0,2,1:T(8,128)(2,1)}, u32[]{:S(2)}) copy-start(bf16[128,1,384]{0,2,1:T(8,128)(2,1)} %copy-done.22) | copy-start | bytes 294916
  51.3 1.6 copy-start.25
  52.0 3.5 %copy-start.21 = (bf16[128,384]{0,1:T(8,128)(2,1)S(1)}, bf16[128,384]{0,1:T(8,128)(2,1)}, u32[]{:S(2)}) copy-start(bf16[128,384]{0,1:T(8,128)(2,1)} %copy-done.20) | copy-start | bytes 294916
  52.3 3.5 %copy-start.13 = (bf16[64,384]{0,1:T(8,128)(2,1)S(1)}, bf16[64,384]{0,1:T(8,128)(2,1)}, u32[]{:S(2)}) copy-start(bf16[64,384]{0,1:T(8,128)(2,1)} %copy-done.12) | copy-start | bytes 147460
  52.3 3.7 %copy-start.15 = (bf16[128,384]{0,1:T(8,128)(2,1)S(1)}, bf16[128,384]{0,1:T(8,128)(2,1)}, u32[]{:S(2)}) copy-start(bf16[128,384]{0,1:T(8,128)(2,1)} %copy-done.14) | copy-start | bytes 294916
  52.6 3.6 %copy-start.9 = (f32[6,64,256]{2,1,0:T(8,128)S(1)}, f32[6,64,256]{2,1,0:T(8,128)}, u32[]{:S(2)}) copy-start(f32[6,64,256]{2,1,0:T(8,128)} %fusion.16) | copy-start | bytes 1179652
  56.5 3.5 %copy-start.32 = (f32[6,64,128]{2,1,0:T(8,128)S(1)}, f32[6,64,128]{2,1,0:T(8,128)}, u32[]{:S(2)}) copy-start(f32[6,64,128]{2,1,0:T(8,128)} %fusion.44) | copy-start | bytes 589828
  58.8 2.2 %copy-start.31 = (f32[6,64,128]{2,1,0:T(8,128)S(1)}, f32[6,64,128]{2,1,0:T(8,128)}, u32[]{:S(2)}) copy-start(f32[6,64,128]{2,1,0:T(8,128)} %fusion.68) | copy-start | bytes 589828
  58.9 99.5 %all-reduce.5.cloned.1.call-start = ((), (), s32[]{:S(2)}) async-start(), calls=%async_computation.1 | async-start | bytes 1179648 | tf_op jit(solution)/shard_map/psum | solution.py:155
  61.7 13.5 %copy-start.39 = (f32[128,384]{1,0:T(8,128)S(1)}, f32[128,384]{1,0:T(8,128)}, u32[]{:S(2)}) copy-start(f32[128,384]{1,0:T(8,128)} %copy.357) | copy-start | bytes 589828
  62.3 54.4 %collective-permute-start.8 = (f32[128,384]{1,0:T(8,128)S(1)}, f32[128,384]{1,0:T(8,128)}, u32[]{:S(2)}, u32[]{:S(2)}) collective-permute-start(f32[128,384]{1,0:T(8,128)S(1)} %copy.351), channel_id=1, source_target_pairs={{0,2},{1,3},{2,0},{3,1},{4,6},{5,7},{6,4},{7,5},{8,10},{9,11},{10,... | collective-permute-start | bytes 589832 | tf_op jit(solution)/shard_map/ppermute | solution.py:10
  64.7 61.2 %collective-permute-start.10 = (f32[128,384]{1,0:T(8,128)S(1)}, f32[128,384]{1,0:T(8,128)}, u32[]{:S(2)}, u32[]{:S(2)}) collective-permute-start(f32[128,384]{1,0:T(8,128)S(1)} %copy.353), channel_id=1, source_target_pairs={{0,1},{1,0},{2,3},{3,2},{4,5},{5,4},{6,7},{7,6},{8,9},{9,8},{10,11... | collective-permute-start | bytes 589832 | tf_op jit(solution)/shard_map/ppermute | solution.py:10
  67.1 59.8 %collective-permute-start.15 = (f32[128,384]{1,0:T(8,128)S(1)}, f32[128,384]{1,0:T(8,128)S(1)}, u32[]{:S(2)}, u32[]{:S(2)}) collective-permute-start(f32[128,384]{1,0:T(8,128)S(1)} %copy.361), channel_id=1, source_target_pairs={{0,1},{1,0},{2,3},{3,2},{4,5},{5,4},{6,7},{7,6},{8,9},{9,8},{10,11... | collective-permute-start | bytes 589832 | tf_op jit(solution)/shard_map/ppermute | solution.py:10
  67.1 8.1 %collective-permute-start.6 = (f32[128,384]{1,0:T(8,128)}, f32[128,384]{1,0:T(8,128)S(1)}, u32[]{:S(2)}, u32[]{:S(2)}) collective-permute-start(f32[128,384]{1,0:T(8,128)} %copy.349), channel_id=1, source_target_pairs={{0,4},{1,5},{2,6},{3,7},{4,0},{5,1},{6,2},{7,3},{8,12},{9,13},{10,... | collective-permute-start | bytes 589832 | tf_op jit(solution)/shard_map/ppermute | solution.py:10
  67.6 53.2 %collective-permute-start.13 = (f32[128,384]{1,0:T(8,128)S(1)}, f32[128,384]{1,0:T(8,128)}, u32[]{:S(2)}, u32[]{:S(2)}) collective-permute-start(f32[128,384]{1,0:T(8,128)S(1)} %copy.359), channel_id=1, source_target_pairs={{0,2},{1,3},{2,0},{3,1},{4,6},{5,7},{6,4},{7,5},{8,10},{9,11},{10,... | collective-permute-start | bytes 589832 | tf_op jit(solution)/shard_map/ppermute | solution.py:10
  75.2 5.6 %collective-permute-start.11 = (f32[128,384]{1,0:T(8,128)S(1)}, f32[128,384]{1,0:T(8,128)S(1)}, u32[]{:S(2)}, u32[]{:S(2)}) collective-permute-start(f32[128,384]{1,0:T(8,128)S(1)} %copy-done.39), channel_id=1, source_target_pairs={{0,4},{1,5},{2,6},{3,7},{4,0},{5,1},{6,2},{7,3},{8,12},{9,13},{10,... | collective-permute-start | bytes 589832 | tf_op jit(solution)/shard_map/ppermute | solution.py:10
  80.8 36.5 %collective-permute-start.7 = (f32[128,384]{1,0:T(8,128)S(1)}, f32[128,384]{1,0:T(8,128)S(1)}, u32[]{:S(2)}, u32[]{:S(2)}) collective-permute-start(f32[128,384]{1,0:T(8,128)S(1)} %select_n.151), channel_id=1, source_target_pairs={{0,2},{1,3},{2,0},{3,1},{4,6},{5,7},{6,4},{7,5},{8,10},{9,11},{10,... | collective-permute-start | bytes 589832 | tf_op jit(solution)/shard_map/ppermute | solution.py:10
  116.8 4.7 %collective-permute-start.12 = (f32[128,384]{1,0:T(8,128)S(1)}, f32[128,384]{1,0:T(8,128)}, u32[]{:S(2)}, u32[]{:S(2)}) collective-permute-start(f32[128,384]{1,0:T(8,128)S(1)} %select_n.159), channel_id=1, source_target_pairs={{0,2},{1,3},{2,0},{3,1},{4,6},{5,7},{6,4},{7,5},{8,10},{9,11},{10,... | collective-permute-start | bytes 589832 | tf_op jit(solution)/shard_map/ppermute | solution.py:10
  118.7 7.2 %collective-permute-start.9 = (f32[128,384]{1,0:T(8,128)S(1)}, f32[128,384]{1,0:T(8,128)S(1)}, u32[]{:S(2)}, u32[]{:S(2)}) collective-permute-start(f32[128,384]{1,0:T(8,128)S(1)} %select_n.155), channel_id=1, source_target_pairs={{0,1},{1,0},{2,3},{3,2},{4,5},{5,4},{6,7},{7,6},{8,9},{9,8},{10,11... | collective-permute-start | bytes 589832 | tf_op jit(solution)/shard_map/ppermute | solution.py:10
  123.0 4.0 %collective-permute-start.14 = (f32[128,384]{1,0:T(8,128)S(1)}, f32[128,384]{1,0:T(8,128)S(1)}, u32[]{:S(2)}, u32[]{:S(2)}) collective-permute-start(f32[128,384]{1,0:T(8,128)S(1)} %select_n.163), channel_id=1, source_target_pairs={{0,1},{1,0},{2,3},{3,2},{4,5},{5,4},{6,7},{7,6},{8,9},{9,8},{10,11... | collective-permute-start | bytes 589832 | tf_op jit(solution)/shard_map/ppermute | solution.py:10
Sparse Core Ops, SparseCore 0:
  59.0 57.7 all-reduce.2
  119.2 39.1 all-reduce.4
